TPU v7x, 512 devices: a whole 4x8x8 slice. The times are simulated.
512 devices in a mesh: shard: 128 (over y, z, core), tensor: 4 (over x).
Axes of the slice: x: 4, y: 8, z: 8, core: 2. Of those that a mesh axis runs over, the one named last changes fastest.
Arguments:
- grads: float32 [256, 384, 384], P('tensor', 'shard'), may hold values from -0.3 to 0.3
- moment_one: float32 [512, 73728], P(('tensor', 'shard')), may hold values from -0.3 to 0.3
- moment_two: float32 [512, 73728], P(('tensor', 'shard')), may hold values from 0.0005 to 0.01
- left_stat: float32 [512, 73728], P(('tensor', 'shard')), may hold values from -1 to 9, as said below
- right_stat: float32 [512, 73728], P(('tensor', 'shard')), may hold values from -1 to 9, as said below
- left_basis: float32 [512, 73728], P(('tensor', 'shard')), may hold values from -1 to 2
- right_basis: float32 [512, 73728], P(('tensor', 'shard')), may hold values from -1 to 2
Outputs:
- update: float32 [256, 384, 384], P('tensor', 'shard')
- new_moment_one: float32 [512, 73728], P(('tensor', 'shard'))
- new_moment_two: float32 [512, 73728], P(('tensor', 'shard'))
- new_left_stat: float32 [512, 73728], P(('tensor', 'shard'))
- new_right_stat: float32 [512, 73728], P(('tensor', 'shard'))
- new_left_basis: float32 [512, 73728], P(('tensor', 'shard'))
- new_right_basis: float32 [512, 73728], P(('tensor', 'shard'))
Inputs may be any that keep to these rules, and one draw needn't show every extreme that they name: `left_stat`: each tile of the statistics is symmetric. `right_stat`: each tile of the statistics is symmetric.
All inputs are finite; a program needn't handle non-finite values.
Results may differ from a plain program's by a relative error of at most 0.00024.
Values sent between devices are 32-bit elements; how exact they have to be, the bound alone decides.
A program may use at most 64 MiB of HBM per device.

v0:
```python
import jax
import jax.numpy as jnp
from jax import lax
from jax.experimental import pallas as pl
from jax.experimental.pallas import tpu as pltpu
from jax.sharding import PartitionSpec as P

NS_ITERS = 5
BETA_ONE = 0.9
BETA_TWO = 0.95
ADAM_EPS = 1e-08
NORM_EPS = 1e-06
LINEAR_COEFF = 3.4445
CUBIC_COEFF = -4.775
QUINTIC_COEFF = 2.0315

B = 384
LINES = 576
MESH = pl.DeviceIdType.MESH
F32 = jnp.float32
BF16 = jnp.bfloat16
NN = (((1,), (0,)), ((), ()))
NT = (((1,), (1,)), ((), ()))


def split(x):
    high = x.astype(BF16)
    return high, (x - high.astype(F32)).astype(BF16)


def dot(a, b, dims=NN):
    left = jnp.concatenate([a[0], a[0], a[1]], dims[0][0][0])
    right = jnp.concatenate([b[0], b[1], b[0]], dims[0][1][0])
    return lax.dot_general(left, right, dims, preferred_element_type=F32)


def every(start, count, stride):
    return pl.ds(start, count, stride=stride)


def swap_halves(x):
    return pltpu.roll(x, 64, 1)


def lower():
    return lax.broadcasted_iota(jnp.int32, (192, 128), 1) < 64


def thirds(ref):
    return ref[every(0, 192, 3), :], ref[every(1, 192, 3), :], ref[every(2, 192, 3), :]


def put_thirds(ref, parts):
    for i in range(3):
        ref[every(i, 192, 3), :] = parts[i]


def whole(ref):
    return jnp.concatenate([ref[i] for i in range(ref.shape[0])], 1)


def put_whole(ref, x):
    for i in range(ref.shape[0]):
        ref[i] = x[:, 128 * i : 128 * i + 128]


def put_half(dst, parts):
    a, b, c = parts
    low = lower()
    zero = jnp.zeros((192, 128), F32)
    even, odd = every(0, 192, 2), every(1, 192, 2)
    cs = swap_halves(c)
    dst[0, even, :] = a
    dst[1, even, :] = jnp.where(low, b, zero)
    dst[0, odd, :] = jnp.where(low, swap_halves(b), cs)
    dst[1, odd, :] = jnp.where(low, cs, zero)


def get_half(src):
    low = lower()
    even, odd = every(0, 192, 2), every(1, 192, 2)
    os = swap_halves(src[0, odd, :])
    return (
        src[0, even, :],
        jnp.where(low, src[1, even, :], os),
        jnp.where(low, os, swap_halves(src[1, odd, :])),
    )


def put_full(dst, first, second):
    a0, b0, c0 = thirds(first)
    a1, b1, c1 = thirds(second)
    low = lower()
    even, odd = every(0, 192, 2), every(1, 192, 2)
    a1s, c0s = swap_halves(a1), swap_halves(c0)
    dst[0, even, :] = a0
    dst[1, even, :] = jnp.where(low, b0, a1s)
    dst[2, even, :] = jnp.where(low, a1s, swap_halves(b1))
    dst[0, odd, :] = jnp.where(low, swap_halves(b0), c0s)
    dst[1, odd, :] = jnp.where(low, c0s, b1)
    dst[2, odd, :] = c1


def flat_full(src, first, second):
    low = lower()
    even, odd = every(0, 192, 2), every(1, 192, 2)
    e0, e1, e2 = (src[i, even, :] for i in range(3))
    o0, o1, o2 = (src[i, odd, :] for i in range(3))
    o0s, e2s = swap_halves(o0), swap_halves(e2)
    put_thirds(first, (e0, jnp.where(low, e1, o0s), jnp.where(low, o0s, swap_halves(o1))))
    put_thirds(second, (jnp.where(low, swap_halves(e1), e2s), jnp.where(low, e2s, o1), o2))


def nth(i):
    return jnp.where((i & 1) == 1, (i + 1) // 2, 8 - i // 2)


def kernel(
    g_in, m1_in, m2_in, ls_in, rs_in, lb_in, rb_in,
    upd_out, nm_out, nv_out, nl_out, nr_out, ql_out, qr_out,
    gs, hop, gbuf, gfull, sraw, lraw, rraw, m1, m2, sfull, qfull, rhalf, work, zbuf, xbuf,
    wp, wr, us, back, pack, ub, upd, nflat, xflat,
    qlh, qll, qth, qtl, qoh, qol,
    lsem, gsem, ssend, srecv, p1s, p1r, p2s, p2r, own, xs, xr, ws, wrv, r1s, r1r, r2s, r2r, ts, tr, osem,
):
    me, t = lax.axis_index("shard"), lax.axis_index("tensor")
    h = me & 1
    chip = me // 2
    cy, cz = chip // 8, chip & 7
    first = h == 0
    a = jnp.where(first, cy, cz)
    b = jnp.where(first, cz, cy)

    def along_one(p):
        return 2 * jnp.where(first, p * 8 + cz, cy * 8 + p) + h

    def along_two(q):
        return 2 * jnp.where(first, cy * 8 + q, q * 8 + cz) + h

    partner = me + 1 - 2 * h

    def remote(src, dst, send, recv, device):
        return pltpu.make_async_remote_copy(
            src_ref=src, dst_ref=dst, send_sem=send, recv_sem=recv, device_id=(device, t), device_id_type=MESH
        )

    barrier = pltpu.get_barrier_semaphore()

    def greet(device):
        pl.semaphore_signal(barrier, inc=1, device_id=(device, t), device_id_type=MESH)

    def greetings(i, carry):
        greet(along_one((a + i) & 7))
        greet(along_two((b + i) & 7))
        return carry

    lax.fori_loop(1, 8, greetings, 0)
    greet(partner)

    def stage(p, carry):
        @pl.when(first)
        def _():
            pltpu.make_async_copy(g_in.at[:, p, :, :], gs.at[p], gsem).start()

        @pl.when(jnp.logical_not(first))
        def _():
            pltpu.make_async_copy(g_in.at[:, :, p, :], gs.at[p], gsem).start()

        return carry

    lax.fori_loop(0, 8, stage, 0)

    @pl.when(first)
    def _():
        pltpu.make_async_copy(ls_in, sraw.at[0], lsem.at[0]).start()

    @pl.when(jnp.logical_not(first))
    def _():
        pltpu.make_async_copy(rs_in, sraw.at[1], lsem.at[0]).start()

    loads = [
        pltpu.make_async_copy(ls_in, sraw.at[h], lsem.at[0]),
        pltpu.make_async_copy(lb_in, lraw.at[h], lsem.at[1]),
        pltpu.make_async_copy(rb_in, rraw.at[h], lsem.at[2]),
        pltpu.make_async_copy(m1_in, m1, lsem.at[3]),
        pltpu.make_async_copy(m2_in, m2, lsem.at[4]),
    ]
    for load in loads[1:]:
        load.start()
    pltpu.make_async_copy(gs, gs, gsem).wait()
    pl.semaphore_wait(barrier, 15)

    def hop_one(i):
        p = (a + i) & 7
        return remote(gs.at[p], hop.at[a], p1s.at[p], p1r.at[a], along_one(p))

    def start_one(i, carry):
        hop_one(nth(8 - i)).start()
        return carry

    lax.fori_loop(1, 8, start_one, 0)

    def forward(src, s):
        def send(i, carry):
            q = (b + nth(8 - i)) & 7
            remote(
                src.at[:, pl.ds(q, 1), :], gbuf.at[h, b, :, pl.ds(s, 1), :], p2s.at[q], p2r.at[b], along_two(q)
            ).start()
            return carry

        lax.fori_loop(1, 8, send, 0)
        pltpu.make_async_copy(src.at[:, pl.ds(b, 1), :], gbuf.at[h, b, :, pl.ds(s, 1), :], own).start()

    forward(gs.at[a], a)

    swaps = [
        remote(lb_in, lraw.at[h], ssend.at[1], srecv.at[1], partner),
        remote(rb_in, rraw.at[h], ssend.at[2], srecv.at[2], partner),
    ]
    for copy in swaps:
        copy.start()

    @pl.when(first)
    def _():
        remote(rs_in, sraw.at[h], ssend.at[0], srecv.at[0], partner).start()

    @pl.when(jnp.logical_not(first))
    def _():
        remote(ls_in, sraw.at[h], ssend.at[0], srecv.at[0], partner).start()

    swap_stat = remote(ls_in, sraw.at[h], ssend.at[0], srecv.at[0], partner)

    def relay(i, carry):
        s = (a + nth(i)) & 7
        remote(gs.at[s], hop.at[s], p1s.at[s], p1r.at[s], along_one(s)).wait_recv()
        forward(hop.at[s], s)
        return carry

    lax.fori_loop(1, 8, relay, 0)

    for load in loads:
        load.wait()
    for copy in swaps:
        copy.wait()
    swap_stat.wait()
    put_full(qfull.at[0], lraw.at[0], lraw.at[1])
    put_full(qfull.at[1], rraw.at[0], rraw.at[1])
    put_full(sfull, sraw.at[0], sraw.at[1])
    put_half(rhalf.at[0], thirds(rraw.at[0]))
    put_half(rhalf.at[1], thirds(rraw.at[1]))
    left = whole(qfull.at[0])
    qlh[...], qll[...] = split(left)
    qth[...], qtl[...] = split(left.T)
    qoh[...], qol[...] = split(whole(qfull.at[h]))

    pltpu.make_async_copy(gbuf.at[0, 0], gbuf.at[0, 0], own).wait()

    def cross(k):
        return remote(gbuf.at[h, k], gbuf.at[h, k], xs.at[k], xr.at[k], partner)

    cross(b).start()

    def pass_on(i, carry):
        k = (b + nth(i)) & 7
        remote(gbuf.at[h, k], gbuf.at[h, k], p2s.at[k], p2r.at[k], along_two(k)).wait_recv()
        cross(k).start()
        return carry

    lax.fori_loop(1, 8, pass_on, 0)

    def crossed(k, carry):
        remote(gbuf.at[1 - h, k], gbuf.at[1 - h, k], xs.at[k], xr.at[k], partner).wait_recv()
        return carry

    lax.fori_loop(0, 8, crossed, 0)
    for k in range(8):
        for r in range(3):
            for c in range(3):
                lanes = pl.ds(128 * c, 128)
                gfull[c, every(6 * k + r, 8, 48), :] = gbuf[0, k, r, :, lanes]
                gfull[c, every(48 * k + 3 + r, 8, 6), :] = gbuf[1, k, r, :, lanes]
    grad = whole(gfull)

    rot = dot((qth[...], qtl[...]), split(dot(split(grad), split(whole(rhalf.at[h])))))
    put_whole(work, rot)
    parts = []
    for i, turned in enumerate(get_half(work)):
        rows = every(i, 192, 3)
        new_first = BETA_ONE * m1[rows, :] + (1.0 - BETA_ONE) * turned
        new_second = BETA_TWO * m2[rows, :] + (1.0 - BETA_TWO) * turned * turned
        m1[rows, :] = new_first
        m2[rows, :] = new_second
        parts.append(new_first / (jnp.sqrt(new_second) + ADAM_EPS))
    stores = [
        pltpu.make_async_copy(m1, nm_out, osem.at[0]),
        pltpu.make_async_copy(m2, nv_out, osem.at[1]),
    ]
    for store in stores:
        store.start()
    put_half(work, parts)
    put_whole(work, dot((qlh[...], qll[...]), split(whole(work))))
    for p in range(8):
        for r in range(3):
            rows = pl.ds((3 * p + r) * 8, 8)
            for c in range(2):
                lanes = pl.ds(128 * c, 128)
                wp[0, rows, lanes] = work[c, every(48 * p + r, 8, 6), :]
                wp[1, rows, lanes] = work[c, every(6 * p + 3 + r, 8, 48), :]
    swap_w = remote(wp.at[1 - h], wr, ws, wrv, partner)
    swap_w.start()

    @pl.when(first)
    def _():
        zbuf[...] = grad

    @pl.when(jnp.logical_not(first))
    def _():
        zbuf[...] = grad.T

    z = split(zbuf[...])
    stat = 0.5 * whole(sfull) + 0.5 * dot(z, z, NT)

    swap_w.wait()
    mine = dot(split(wp[h]), split(whole(rhalf.at[h])), NT)
    us[...] = (mine + dot(split(wr[...]), split(whole(rhalf.at[1 - h])), NT)).reshape(8, 3, 8, B)

    def back_one(i):
        p = (a + i) & 7
        return remote(us.at[p], back.at[a], r1s.at[p], r1r.at[a], along_one(p))

    def start_back(i, carry):
        back_one(nth(8 - i)).start()
        return carry

    lax.fori_loop(1, 8, start_back, 0)
    keep = pltpu.make_async_copy(us.at[a], back.at[a], own)
    keep.start()

    put_whole(sfull, stat)
    power = dot(split(stat), (qoh[...], qol[...]))
    scale = 1.0 / jnp.sqrt(jnp.sum(power * power) + NORM_EPS)
    x = power * scale
    flat_full(sfull, nflat.at[0], nflat.at[1])

    def halves_out(flat, left_out, right_out, sem, send, recv):
        @pl.when(first)
        def _():
            pltpu.make_async_copy(flat.at[0], left_out, sem).start()
            remote(flat.at[1], left_out, send, recv, partner).start()

        @pl.when(jnp.logical_not(first))
        def _():
            pltpu.make_async_copy(flat.at[1], right_out, sem).start()
            remote(flat.at[0], right_out, send, recv, partner).start()

    def halves_wait(flat, left_out, right_out, sem, send, recv):
        pltpu.make_async_copy(flat.at[0], left_out, sem).wait()

        @pl.when(first)
        def _():
            remote(flat.at[1], right_out, send, recv, partner).wait()

        @pl.when(jnp.logical_not(first))
        def _():
            remote(flat.at[0], left_out, send, recv, partner).wait()

    halves_out(nflat, nl_out, nr_out, osem.at[2], ts.at[0], tr.at[0])

    def quintic(x):
        parts = split(x)
        gram = dot(parts, parts, NT)
        g = split(gram)
        poly = CUBIC_COEFF * gram + QUINTIC_COEFF * dot(g, g)
        return LINEAR_COEFF * x + dot(split(poly), parts)

    x = quintic(quintic(x))

    def landed(i, carry):
        s = (a + i) & 7
        remote(us.at[s], back.at[s], r1s.at[s], r1r.at[s], along_one(s)).wait()
        return carry

    lax.fori_loop(1, 8, landed, 0)
    keep.wait()
    for s in range(8):
        for r in range(3):
            for c in range(3):
                pack[c, every(r * 8 + s, 8, 24), :] = back[s, r, :, 128 * c : 128 * c + 128]

    def back_two(i):
        q = (b + i) & 7
        return remote(pack.at[:, pl.ds(pl.multiple_of(q * 24, 8), 24), :], ub.at[b], r2s.at[q], r2r.at[b], along_two(q))

    def start_two(i, carry):
        back_two(nth(8 - i)).start()
        return carry

    lax.fori_loop(1, 8, start_two, 0)
    keep_two = pltpu.make_async_copy(pack.at[:, pl.ds(pl.multiple_of(b * 24, 8), 24), :], ub.at[b], own)
    keep_two.start()

    x = quintic(quintic(quintic(x)))
    put_whole(xbuf, x)
    flat_full(xbuf, xflat.at[0], xflat.at[1])
    halves_out(xflat, ql_out, qr_out, osem.at[3], ts.at[1], tr.at[1])

    def arrived(i, carry):
        q = (b + i) & 7
        remote(
            pack.at[:, pl.ds(pl.multiple_of(q * 24, 8), 24), :], ub.at[q], r2s.at[q], r2r.at[q], along_two(q)
        ).wait()
        return carry

    lax.fori_loop(1, 8, arrived, 0)
    keep_two.wait()

    @pl.when(first)
    def _():
        for k in range(8):
            for r in range(3):
                for c in range(3):
                    upd[c, every(64 * r + k, 8, 8), :] = ub[k, c, pl.ds(8 * r, 8), :]

    @pl.when(jnp.logical_not(first))
    def _():
        for k in range(8):
            for r in range(3):
                for c in range(3):
                    upd[c, pl.ds(64 * r + 8 * k, 8), :] = ub[k, c, pl.ds(8 * r, 8), :]

    lasts = [
        pltpu.make_async_copy(upd.at[c], upd_out.at[:, pl.ds(128 * c, 128)], osem.at[4 + c]) for c in range(3)
    ]
    for last in lasts:
        last.start()

    def sent(i, carry):
        p = (a + i) & 7
        q = (b + i) & 7
        remote(gs.at[p], hop.at[a], p1s.at[p], p1r.at[a], along_one(p)).wait_send()
        remote(gbuf.at[h, q], gbuf.at[h, q], p2s.at[q], p2r.at[q], along_two(q)).wait_send()
        return carry

    lax.fori_loop(1, 8, sent, 0)

    def sent_cross(k, carry):
        cross(k).wait_send()
        return carry

    lax.fori_loop(0, 8, sent_cross, 0)
    for store in stores:
        store.wait()
    halves_wait(nflat, nl_out, nr_out, osem.at[2], ts.at[0], tr.at[0])
    halves_wait(xflat, ql_out, qr_out, osem.at[3], ts.at[1], tr.at[1])
    for last in lasts:
        last.wait()


def step(grads, *flats):
    tiles = (LINES, 128)
    square = (B, B)
    dma = pltpu.SemaphoreType.DMA
    scratch = [
        pltpu.VMEM((8, 3, 8, B), F32),
        pltpu.VMEM((8, 3, 8, B), F32),
        pltpu.VMEM((2, 8, 3, 8, B), F32),
        pltpu.VMEM((3, B, 128), F32),
        pltpu.VMEM((2, *tiles), F32),
        pltpu.VMEM((2, *tiles), F32),
        pltpu.VMEM((2, *tiles), F32),
        pltpu.VMEM(tiles, F32),
        pltpu.VMEM(tiles, F32),
        pltpu.VMEM((3, B, 128), F32),
        pltpu.VMEM((2, 3, B, 128), F32),
        pltpu.VMEM((2, 2, B, 128), F32),
        pltpu.VMEM((2, B, 128), F32),
        pltpu.VMEM(square, F32),
        pltpu.VMEM((3, B, 128), F32),
        pltpu.VMEM((2, 192, 256), F32),
        pltpu.VMEM((192, 256), F32),
        pltpu.VMEM((8, 3, 8, B), F32),
        pltpu.VMEM((8, 3, 8, B), F32),
        pltpu.VMEM((3, 192, 128), F32),
        pltpu.VMEM((8, 3, 24, 128), F32),
        pltpu.VMEM((3, 192, 128), F32),
        pltpu.VMEM((2, *tiles), F32),
        pltpu.VMEM((2, *tiles), F32),
        *[pltpu.VMEM(square, BF16)] * 6,
        dma((5,)),
        dma,
        dma((3,)),
        dma((3,)),
        *[dma((8,))] * 4,
        dma,
        *[dma((8,))] * 2,
        *[dma] * 2,
        *[dma((8,))] * 4,
        *[dma((2,))] * 2,
        dma((7,)),
    ]
    anywhere = pl.BlockSpec(memory_space=pl.ANY)
    flat = jax.ShapeDtypeStruct(tiles, F32)
    outs = pl.pallas_call(
        kernel,
        out_shape=(jax.ShapeDtypeStruct((192, B), F32), *[flat] * 6),
        in_specs=[anywhere] * 7,
        out_specs=(anywhere,) * 7,
        scratch_shapes=scratch,
        compiler_params=pltpu.CompilerParams(collective_id=0, has_side_effects=True, vmem_limit_bytes=60 << 20),
        name="soap_step",
    )(grads.transpose(1, 0, 2).reshape(3, 8, 8, B), *[x.reshape(tiles) for x in flats])
    return (outs[0].reshape(3, 64, B).transpose(1, 0, 2), *[x.reshape(1, -1) for x in outs[1:]])


def solution(mesh):
    specs = (P("tensor", "shard", None), *[P(("tensor", "shard"), None)] * 6)
    return jax.shard_map(step, mesh=mesh, in_specs=specs, out_specs=specs, check_vma=False)
```

profile of v0, /device:TPU:1, one launch (start us, length us, event | category | flops | bytes accessed | tf_op | source)
XLA Modules:
  0.0 55.5 jit_solution(4138697569309735265)
XLA Ops:
  0.6 47.0 %soap_step.1 = (f32[192,384]{1,0:T(8,128)}, f32[576,128]{1,0:T(8,128)}, f32[576,128]{1,0:T(8,128)}, f32[576,128]{1,0:T(8,128)}, f32[576,128]{1,0:T(8,128)}, /*index=5*/f32[576,128]{1,0:T(8,128)}, f32[576,128]{1,0:T(8,128)}) custom-call(f32[3,8,8,384]{3,2,1,0:T(8,128)} %bitcast.25, f32[576,128]{1,0:T(8,128)} %bitcast.26, f32[576,128]{1,0:T(8,128)} %bitcast.27, ...), custom_call_target="tpu_custom_call" | custom-call | tf_op jit(solution)/shard_map/soap_step/pallas_call | solution.py:503
  47.6 0.0 copy-start.5
  47.7 1.7 %copy.21 = f32[64,3,384]{2,0,1:T(8,128)} copy(f32[64,3,384]{2,0,1:T(8,128)} %bitcast.24) | data formatting | bytes 589824
  49.4 0.0 copy-done.5
  49.4 0.0 copy-start.4
  49.4 0.7 %copy.22 = f32[1,73728]{1,0:T(1,128)} copy(f32[1,73728]{1,0:T(1,128)S(1)} %bitcast.23) | data formatting | bytes 589824
  50.1 0.4 copy-done.4
  50.5 0.0 copy-start.3
  50.5 0.7 %copy.23 = f32[1,73728]{1,0:T(1,128)} copy(f32[1,73728]{1,0:T(1,128)S(1)} %bitcast.22) | data formatting | bytes 589824
  51.2 0.4 copy-done.3
  51.5 0.0 copy-start.2
  51.5 0.7 %copy.24 = f32[1,73728]{1,0:T(1,128)} copy(f32[1,73728]{1,0:T(1,128)S(1)} %bitcast.21) | data formatting | bytes 589824
  52.3 0.4 copy-done.2
  52.6 0.0 copy-start.1
  52.6 0.7 %copy.25 = f32[1,73728]{1,0:T(1,128)} copy(f32[1,73728]{1,0:T(1,128)S(1)} %bitcast.20) | data formatting | bytes 589824
  53.3 0.4 copy-done.1
  53.7 0.0 copy-start
  53.7 0.7 %copy.26 = f32[1,73728]{1,0:T(1,128)} copy(f32[1,73728]{1,0:T(1,128)S(1)} %bitcast.19) | data formatting | bytes 589824
  54.4 0.4 copy-done
  54.7 0.7 %copy.27 = f32[1,73728]{1,0:T(1,128)} copy(f32[1,73728]{1,0:T(1,128)S(1)} %bitcast.18) | data formatting | bytes 589824
Async XLA Ops:
  47.6 1.8 %copy-start.5 = (f32[576,128]{1,0:T(8,128)S(1)}, f32[576,128]{1,0:T(8,128)}, u32[]{:S(2)}) copy-start(f32[576,128]{1,0:T(8,128)} %get-tuple-element.15) | copy-start | bytes 884740
  49.4 1.1 %copy-start.4 = (f32[576,128]{1,0:T(8,128)S(1)}, f32[576,128]{1,0:T(8,128)}, u32[]{:S(2)}) copy-start(f32[576,128]{1,0:T(8,128)} %get-tuple-element.16) | copy-start | bytes 884740
  50.5 1.1 %copy-start.3 = (f32[576,128]{1,0:T(8,128)S(1)}, f32[576,128]{1,0:T(8,128)}, u32[]{:S(2)}) copy-start(f32[576,128]{1,0:T(8,128)} %get-tuple-element.17) | copy-start | bytes 884740
  51.5 1.1 %copy-start.2 = (f32[576,128]{1,0:T(8,128)S(1)}, f32[576,128]{1,0:T(8,128)}, u32[]{:S(2)}) copy-start(f32[576,128]{1,0:T(8,128)} %get-tuple-element.18) | copy-start | bytes 884740
  52.6 1.1 %copy-start.1 = (f32[576,128]{1,0:T(8,128)S(1)}, f32[576,128]{1,0:T(8,128)}, u32[]{:S(2)}) copy-start(f32[576,128]{1,0:T(8,128)} %get-tuple-element.19) | copy-start | bytes 884740
  53.7 1.1 %copy-start = (f32[576,128]{1,0:T(8,128)S(1)}, f32[576,128]{1,0:T(8,128)}, u32[]{:S(2)}) copy-start(f32[576,128]{1,0:T(8,128)} %get-tuple-element.20) | copy-start | bytes 884740
where the time goes:
time: 55.8 us; the launch traced here: 55.5 us
  Pallas kernels  47 us (84%)
  local copies, waits for them, and re-layouts  7.8 us (14%)
  between operations  0.66 us (1%)
    pallas_call x1, Pallas kernels, step(): pl.pallas_call(kernel, out_shape=(jax.ShapeDtypeStruct((192, B), F32), *[...  47 us
    unnamed x19, local copies, waits for them, and re-layouts  7.8 us

commit v1 on v0

--- a/solution.py
+++ b/solution.py
@@ -16,6 +16,7 @@
 
 B = 384
 LINES = 576
+VMEM_BYTES = 30 << 20
 MESH = pl.DeviceIdType.MESH
 F32 = jnp.float32
 BF16 = jnp.bfloat16
@@ -454,6 +455,14 @@
     halves_wait(xflat, ql_out, qr_out, osem.at[3], ts.at[1], tr.at[1])
     for last in lasts:
         last.wait()
+
+
+def hand_out(*refs):
+    copies = [pltpu.make_async_copy(refs[i], refs[7 + i], refs[14].at[i]) for i in range(7)]
+    for copy in copies:
+        copy.start()
+    for copy in copies:
+        copy.wait()
 
 
 def step(grads, *flats):
@@ -498,17 +507,27 @@
         *[dma((2,))] * 2,
         dma((7,)),
     ]
-    anywhere = pl.BlockSpec(memory_space=pl.ANY)
-    flat = jax.ShapeDtypeStruct(tiles, F32)
+    inside = pl.BlockSpec(memory_space=pltpu.VMEM)
+    outside = pl.BlockSpec(memory_space=pltpu.HBM)
+    shapes = (jax.ShapeDtypeStruct((192, B), F32), *[jax.ShapeDtypeStruct(tiles, F32)] * 6)
+    held = pl.pallas_call(
+        kernel,
+        out_shape=shapes,
+        in_specs=[outside] * 7,
+        out_specs=(inside,) * 7,
+        scratch_shapes=scratch,
+        compiler_params=pltpu.CompilerParams(collective_id=0, has_side_effects=True, vmem_limit_bytes=VMEM_BYTES),
+        name="soap_step",
+    )(*[pltpu.with_memory_space_constraint(x, pltpu.HBM) for x in (grads.transpose(1, 0, 2).reshape(3, 8, 8, B), *[x.reshape(tiles) for x in flats])])
     outs = pl.pallas_call(
-        kernel,
-        out_shape=(jax.ShapeDtypeStruct((192, B), F32), *[flat] * 6),
-        in_specs=[anywhere] * 7,
-        out_specs=(anywhere,) * 7,
-        scratch_shapes=scratch,
-        compiler_params=pltpu.CompilerParams(collective_id=0, has_side_effects=True, vmem_limit_bytes=60 << 20),
-        name="soap_step",
-    )(grads.transpose(1, 0, 2).reshape(3, 8, 8, B), *[x.reshape(tiles) for x in flats])
+        hand_out,
+        out_shape=shapes,
+        in_specs=[inside] * 7,
+        out_specs=(outside,) * 7,
+        scratch_shapes=[dma((7,))],
+        compiler_params=pltpu.CompilerParams(vmem_limit_bytes=VMEM_BYTES),
+        name="hand_out",
+    )(*held)
     return (outs[0].reshape(3, 64, B).transpose(1, 0, 2), *[x.reshape(1, -1) for x in outs[1:]])
 
 

time: 55.8 us -> 49.3 us (0.88)
  local copies, waits for them, and re-layouts: 7.8 us -> 0 us
  Pallas kernels: 47 us -> 48.5 us
    unnamed x19 -> x0, local copies, waits for them, and re-layouts: 7.8 us -> none
    pallas_call x1 -> x2, Pallas kernels: 47 us -> 48.5 us  [the longest x1 47.1 us: step(): pl.pallas_call(kernel, out_shape=shapes, in_specs=[outside] * 7, out_spec...]
where the time goes in v1:
time: 49.3 us; the launch traced here: 49.1 us
  Pallas kernels  48.5 us (98%)
  between operations  0.64 us (1%)
    pallas_call x1, Pallas kernels, step(): pl.pallas_call(kernel, out_shape=shapes, in_specs=[outside] * 7, out_spec...  47.1 us
    pallas_call x1, Pallas kernels, step(): pl.pallas_call(hand_out, out_shape=shapes, in_specs=[inside] * 7, out_spe...  1.36 us

profile of v1, /device:TPU:1, one launch (start us, length us, event | category | flops | bytes accessed | tf_op | source)
XLA Modules:
  0.0 49.1 jit_solution(9260609239533444931)
XLA Ops:
  0.6 47.1 %soap_step.1 = (f32[192,384]{1,0:T(8,128)S(1)}, f32[576,128]{1,0:T(8,128)S(1)}, f32[576,128]{1,0:T(8,128)S(1)}, f32[576,128]{1,0:T(8,128)S(1)}, f32[576,128]{1,0...) custom-call(f32[3,8,8,384]{3,2,1,0:T(8,128)} %bitcast.18, f32[576,128]{1,0:T(8,128)} %bitcast.19, ...), custom_call_target="tpu_custom_call" | custom-call | tf_op jit(solution)/shard_map/soap_step/pallas_call | solution.py:513
  47.8 1.4 %hand_out.1 = (f32[192,384]{1,0:T(8,128)}, f32[576,128]{1,0:T(8,128)}, f32[576,128]{1,0:T(8,128)}, f32[576,128]{1,0:T(8,128)}, f32[576,128]{1,0:T(8,128)}, /*index=5*/f32[576,128]{1,0:T(8,128)}, f32[576,128]{1,0:T(8,128)}) custom-call(f32[192,384]{1,0:T(8,128)S(1)} %get-tuple-element.21.refs_0_, f32[576,128]{1,0:T(8,128)S(1)} %get-tuple-element.22.refs_1_, ...), custom_call_target="tpu_custom_call" | custom-call | tf_op jit(solution)/shard_map/hand_out/pallas_call | solution.py:522

commit v2 on v1

--- a/solution.py
+++ b/solution.py
@@ -33,6 +33,14 @@
     left = jnp.concatenate([a[0], a[0], a[1]], dims[0][0][0])
     right = jnp.concatenate([b[0], b[1], b[0]], dims[0][1][0])
     return lax.dot_general(left, right, dims, preferred_element_type=F32)
+
+
+def symmetric(a, dims):
+    cut = 256
+    inner = tuple(x[:cut] if dims is NT else x[:, :cut] for x in a)
+    corner = dot(tuple(x[:cut] for x in a), inner, dims)
+    rows = dot(tuple(x[cut:] for x in a), a, dims)
+    return jnp.concatenate([jnp.concatenate([corner, rows[:, :cut].T], 1), rows], 0)
 
 
 def every(start, count, stride):
@@ -119,7 +127,7 @@
 def kernel(
     g_in, m1_in, m2_in, ls_in, rs_in, lb_in, rb_in,
     upd_out, nm_out, nv_out, nl_out, nr_out, ql_out, qr_out,
-    gs, hop, gbuf, gfull, sraw, lraw, rraw, m1, m2, sfull, qfull, rhalf, work, zbuf, xbuf,
+    gs, hop, gbuf, gfull, sraw, lraw, rraw, m1, m2, sfull, qfull, rhalf, work, zhigh, zlow, xbuf,
     wp, wr, us, back, pack, ub, upd, nflat, xflat,
     qlh, qll, qth, qtl, qoh, qol,
     lsem, gsem, ssend, srecv, p1s, p1r, p2s, p2r, own, xs, xr, ws, wrv, r1s, r1r, r2s, r2r, ts, tr, osem,
@@ -280,9 +288,9 @@
                 lanes = pl.ds(128 * c, 128)
                 gfull[c, every(6 * k + r, 8, 48), :] = gbuf[0, k, r, :, lanes]
                 gfull[c, every(48 * k + 3 + r, 8, 6), :] = gbuf[1, k, r, :, lanes]
-    grad = whole(gfull)
-
-    rot = dot((qth[...], qtl[...]), split(dot(split(grad), split(whole(rhalf.at[h])))))
+    grad_parts = split(whole(gfull))
+
+    rot = dot((qth[...], qtl[...]), split(dot(grad_parts, split(whole(rhalf.at[h])))))
     put_whole(work, rot)
     parts = []
     for i, turned in enumerate(get_half(work)):
@@ -312,14 +320,14 @@
 
     @pl.when(first)
     def _():
-        zbuf[...] = grad
+        zhigh[...], zlow[...] = grad_parts
 
     @pl.when(jnp.logical_not(first))
     def _():
-        zbuf[...] = grad.T
-
-    z = split(zbuf[...])
-    stat = 0.5 * whole(sfull) + 0.5 * dot(z, z, NT)
+        zhigh[...], zlow[...] = grad_parts[0].T, grad_parts[1].T
+
+    z = zhigh[...], zlow[...]
+    stat = 0.5 * whole(sfull) + 0.5 * symmetric(z, NT)
 
     swap_w.wait()
     mine = dot(split(wp[h]), split(whole(rhalf.at[h])), NT)
@@ -369,12 +377,11 @@
 
     def quintic(x):
         parts = split(x)
-        gram = dot(parts, parts, NT)
-        g = split(gram)
-        poly = CUBIC_COEFF * gram + QUINTIC_COEFF * dot(g, g)
+        gram = symmetric(parts, NT)
+        poly = CUBIC_COEFF * gram + QUINTIC_COEFF * symmetric(split(gram), NN)
         return LINEAR_COEFF * x + dot(split(poly), parts)
 
-    x = quintic(quintic(x))
+    x = quintic(quintic(quintic(x)))
 
     def landed(i, carry):
         s = (a + i) & 7
@@ -400,10 +407,29 @@
     keep_two = pltpu.make_async_copy(pack.at[:, pl.ds(pl.multiple_of(b * 24, 8), 24), :], ub.at[b], own)
     keep_two.start()
 
-    x = quintic(quintic(quintic(x)))
+    x = quintic(quintic(x))
     put_whole(xbuf, x)
     flat_full(xbuf, xflat.at[0], xflat.at[1])
     halves_out(xflat, ql_out, qr_out, osem.at[3], ts.at[1], tr.at[1])
+
+    def sent(i, carry):
+        p = (a + i) & 7
+        q = (b + i) & 7
+        remote(gs.at[p], hop.at[a], p1s.at[p], p1r.at[a], along_one(p)).wait_send()
+        remote(gbuf.at[h, q], gbuf.at[h, q], p2s.at[q], p2r.at[q], along_two(q)).wait_send()
+        return carry
+
+    lax.fori_loop(1, 8, sent, 0)
+
+    def sent_cross(k, carry):
+        cross(k).wait_send()
+        return carry
+
+    lax.fori_loop(0, 8, sent_cross, 0)
+    for store in stores:
+        store.wait()
+    halves_wait(nflat, nl_out, nr_out, osem.at[2], ts.at[0], tr.at[0])
+
 
     def arrived(i, carry):
         q = (b + i) & 7
@@ -435,23 +461,6 @@
     for last in lasts:
         last.start()
 
-    def sent(i, carry):
-        p = (a + i) & 7
-        q = (b + i) & 7
-        remote(gs.at[p], hop.at[a], p1s.at[p], p1r.at[a], along_one(p)).wait_send()
-        remote(gbuf.at[h, q], gbuf.at[h, q], p2s.at[q], p2r.at[q], along_two(q)).wait_send()
-        return carry
-
-    lax.fori_loop(1, 8, sent, 0)
-
-    def sent_cross(k, carry):
-        cross(k).wait_send()
-        return carry
-
-    lax.fori_loop(0, 8, sent_cross, 0)
-    for store in stores:
-        store.wait()
-    halves_wait(nflat, nl_out, nr_out, osem.at[2], ts.at[0], tr.at[0])
     halves_wait(xflat, ql_out, qr_out, osem.at[3], ts.at[1], tr.at[1])
     for last in lasts:
         last.wait()
@@ -483,7 +492,7 @@
         pltpu.VMEM((2, 3, B, 128), F32),
         pltpu.VMEM((2, 2, B, 128), F32),
         pltpu.VMEM((2, B, 128), F32),
-        pltpu.VMEM(square, F32),
+        *[pltpu.VMEM(square, BF16)] * 2,
         pltpu.VMEM((3, B, 128), F32),
         pltpu.VMEM((2, 192, 256), F32),
         pltpu.VMEM((192, 256), F32),

time: 49.3 us -> 47.4 us (0.961)
  Pallas kernels: 48.5 us -> 46.6 us
    pallas_call x1, Pallas kernels: 47.1 us -> 45.3 us  [step(): pl.pallas_call(kernel, out_shape=shapes, in_specs=[outside] * 7, out_spec...]
where the time goes in v2:
time: 47.4 us; the launch traced here: 47.3 us
  Pallas kernels  46.6 us (98%)
  between operations  0.64 us (1%)
    pallas_call x1, Pallas kernels, step(): pl.pallas_call(kernel, out_shape=shapes, in_specs=[outside] * 7, out_spec...  45.3 us
    pallas_call x1, Pallas kernels, step(): pl.pallas_call(hand_out, out_shape=shapes, in_specs=[inside] * 7, out_spe...  1.36 us

profile of v2, /device:TPU:1, one launch (start us, length us, event | category | flops | bytes accessed | tf_op | source)
XLA Modules:
  0.0 47.3 jit_solution(2061211921644551100)
XLA Ops:
  0.6 45.3 %soap_step.1 = (f32[192,384]{1,0:T(8,128)S(1)}, f32[576,128]{1,0:T(8,128)S(1)}, f32[576,128]{1,0:T(8,128)S(1)}, f32[576,128]{1,0:T(8,128)S(1)}, f32[576,128]{1,0...) custom-call(f32[3,8,8,384]{3,2,1,0:T(8,128)} %bitcast.18, f32[576,128]{1,0:T(8,128)} %bitcast.19, ...), custom_call_target="tpu_custom_call" | custom-call | tf_op jit(solution)/shard_map/soap_step/pallas_call | solution.py:522
  45.9 1.4 %hand_out.1 = (f32[192,384]{1,0:T(8,128)}, f32[576,128]{1,0:T(8,128)}, f32[576,128]{1,0:T(8,128)}, f32[576,128]{1,0:T(8,128)}, f32[576,128]{1,0:T(8,128)}, /*index=5*/f32[576,128]{1,0:T(8,128)}, f32[576,128]{1,0:T(8,128)}) custom-call(f32[192,384]{1,0:T(8,128)S(1)} %get-tuple-element.21.refs_0_, f32[576,128]{1,0:T(8,128)S(1)} %get-tuple-element.22.refs_1_, ...), custom_call_target="tpu_custom_call" | custom-call | tf_op jit(solution)/shard_map/hand_out/pallas_call | solution.py:531
